TPU v7x, 32 devices: a whole 2x2x4 slice. The times are simulated.
32 devices in a mesh: blk: 8 (over z, x), pair: 4 (over y, core).
Axes of the slice: x: 2, y: 2, z: 4, core: 2. Of those that a mesh axis runs over, the one named last changes fastest.
Arguments:
- records: bfloat16 [8, 1024, 2048], P('blk', 'pair'), may hold values from -100 to 100
- offsets: int32 [2], replicated, may hold values from 1 to 7, as said below
- source_side: int32 [8, 2], P('blk'), may hold values from 0 to 1
Outputs:
- first_side: bfloat16 [8, 2, 32, 128, 128], P('blk', None, 'pair')
- second_side: bfloat16 [8, 2, 32, 128, 128], P('blk', None, 'pair')
Inputs may be any that keep to these rules, and one draw needn't show every extreme that they name: `offsets`: distinct and increasing; the last one is 7.
All inputs are finite; a program needn't handle non-finite values.
Results may differ from a plain program's by a relative error of at most 0.012.
Values may be sent and summed in bfloat16 or wider, within the bound.
No kernel may reach another device: no remote copies, remote signals or barrier semaphores. Data moves between devices by JAX's collectives and lax.ppermute only.
A program may use at most 128 MiB of HBM per device.

v0:
```python
import math
import jax
import jax.numpy as jnp
from jax import lax
from jax.sharding import PartitionSpec as P

BLOCK_CH = 128
BINS = 128
SAMPLES = 2048
FIRST_BIN = 4
LAGS = 32


def as_sent(value):
    return jax.tree.map(lambda a: a.astype(jnp.bfloat16) if a.dtype == jnp.float32 else a, value)


def shifted_2(value, axis, steps):
    count = lax.axis_size(axis)
    leading, last = (max(0, -steps), min(count, count - steps))
    return lax.ppermute(value, axis, [(source, source + steps) for source in range(leading, last)])


def fourier_table():
    sample_index = jnp.arange(SAMPLES, dtype=jnp.int32)
    bin_index = FIRST_BIN + jnp.arange(BINS, dtype=jnp.int32)
    phase_index = sample_index[:, None] * bin_index[None, :] % SAMPLES
    angles = 2.0 * math.pi / SAMPLES * phase_index.astype(jnp.float32)
    hann_taper = 0.5 - 0.5 * jnp.cos(2.0 * math.pi / SAMPLES * sample_index.astype(jnp.float32))
    return jnp.stack(
        (hann_taper[:, None] * jnp.cos(angles), -hann_taper[:, None] * jnp.sin(angles)), axis=-1
    )


def shift_ahead(distance):
    return lambda block: jax.tree.map(
        lambda part, own: part.astype(own.dtype), shifted_2(as_sent(block), "blk", -distance), block
    )


def local(records, offsets, source_side):
    seg_local = records.shape[0]
    local_blocks = records.shape[1] // BLOCK_CH
    table_full = fourier_table()
    table_high = lax.optimization_barrier(table_full.astype(jnp.bfloat16))
    table_low = (table_full - table_high.astype(jnp.float32)).astype(jnp.bfloat16)
    traces = records.reshape(seg_local, local_blocks, BLOCK_CH, SAMPLES)
    spectrum = jnp.einsum("sbcn,nfr->bfsrc", traces, table_high, preferred_element_type=jnp.float32)
    spectrum = spectrum + jnp.einsum(
        "sbcn,nfr->bfsrc", traces, table_low, preferred_element_type=jnp.float32
    )
    band_power = jnp.sum(spectrum * spectrum, axis=3)
    band_level = jnp.mean(band_power, axis=-1)
    whiten_scale = 1.0 / jnp.sqrt(band_level + 1e-05)
    whitened = (spectrum * whiten_scale[:, :, :, None, None]).astype(jnp.bfloat16)
    regrouped = lax.all_to_all(
        lax.all_to_all(whitened, "pair", split_axis=1, concat_axis=0, tiled=True),
        "blk",
        split_axis=0,
        concat_axis=2,
        tiled=True,
    )
    own_block = regrouped[0]
    bin_local = own_block.shape[0]
    seg_total = own_block.shape[1]
    offset_total = offsets.shape[0]
    group_size = lax.axis_size("blk")
    window_size = min(16, group_size)
    bit_total = window_size.bit_length() - 1
    ahead_list = [shift_ahead(distance) for distance in range(1, window_size)]
    partners = jnp.stack(
        [lax.switch(offsets[slot] - 1, ahead_list, own_block) for slot in range(offset_total)]
    )
    reverse_side = (source_side[0] == 1)[:, None, None, None, None]
    own_many = jnp.broadcast_to(own_block[None], partners.shape)
    source = jnp.where(reverse_side, partners, own_many)
    receiver = jnp.where(reverse_side, own_many, partners)
    left_side = source.reshape(offset_total, bin_local, 2 * seg_total, BLOCK_CH)
    rotated = jnp.stack((receiver[:, :, :, 1], -receiver[:, :, :, 0]), axis=3)
    right_side = jnp.stack((receiver, rotated), axis=4).reshape(
        offset_total, bin_local, 2 * seg_total, 2, BLOCK_CH
    )
    cross = jnp.einsum(
        "kfsc,kfsrd->kfrcd", left_side, right_side, preferred_element_type=jnp.float32
    )
    cross_rows = cross.reshape(offset_total, 2 * bin_local, BLOCK_CH * BLOCK_CH)
    pair_index = lax.axis_index("pair")
    lag_index = jnp.arange(LAGS, dtype=jnp.int32) - LAGS // 2
    bin_index = FIRST_BIN + pair_index * bin_local + jnp.arange(bin_local, dtype=jnp.int32)
    phase_index = lag_index[:, None] * bin_index[None, :] % SAMPLES
    angles = 2.0 * math.pi / SAMPLES * phase_index.astype(jnp.float32)
    normalizer = 1.0 / math.sqrt(seg_total * BINS)
    lag_table = (jnp.stack((jnp.cos(angles), -jnp.sin(angles)), axis=-1) * normalizer).reshape(
        LAGS, 2 * bin_local
    )
    summed = lax.psum_scatter(
        jnp.einsum(
            "lq,kqx->lkx",
            lag_table,
            cross_rows,
            precision=lax.Precision.HIGHEST,
            preferred_element_type=jnp.float32,
        ).astype(jnp.bfloat16),
        "pair",
        scatter_dimension=0,
        tiled=True,
    ).astype(jnp.float32)
    lag_local = summed.shape[0]
    first_local = (
        summed.astype(jnp.bfloat16)
        .transpose(1, 0, 2)
        .reshape(offset_total, lag_local, BLOCK_CH, BLOCK_CH)
    )
    returned = first_local
    for bit_number in range(bit_total):
        shifted = shifted_2(returned, "blk", 1 << bit_number)
        selected = (jnp.right_shift(offsets, bit_number) % 2 == 1)[:, None, None, None]
        returned = jnp.where(selected, shifted, returned)
    return (first_local[None], returned[None])


def solution(mesh):
    placed = (P("blk", "pair", None), P(), P("blk", None))
    return jax.shard_map(
        local,
        mesh=mesh,
        in_specs=placed,
        out_specs=(P("blk", None, "pair", None, None), P("blk", None, "pair", None, None)),
        check_vma=False,
    )
```

profile of v0, /device:TPU:25, one launch (start us, length us, event | category | flops | bytes accessed | tf_op | source)
XLA Modules:
  0.0 181.7 jit_solution(7638834543979147514)
XLA Ops:
  7.2 4.2 %cosine_multiply_fusion = (f32[2048,128,1]{1,0,2:T(8,128)S(1)}, f32[2048,128,1]{1,0,2:T(8,128)S(1)}) fusion(s32[128]{0:T(128)S(1)} %iota_add_fusion, f32[2048]{0:T(1024)S(1)} %get-tuple-element.57, f32[2048]{0:T(1024)S(1)} %get-tuple-element.58), kind=kLoop, calls=%fused_computation.18 | loop fusion | flops 4194304 | bytes 2114048 | tf_op jit(solution)/shard_map/mul | solution.py:31
  13.4 4.0 %all-to-all-start = ((bf16[2,128,1,2,128]{4,0,3,2,1:T(2,128)(2,1)}), bf16[2,128,1,2,128]{4,0,3,2,1:T(2,128)(2,1)S(1)}, u32[]{:S(2)}, u32[]{:S(2)}) async-start(bf16[2,128,1,2,128]{4,0,3,2,1:T(2,128)(2,1)} %copy.65), calls=%async_computation | async-start | bytes 262144 | tf_op jit(solution)/shard_map/all_to_all | solution.py:57
  17.6 3.4 %all-to-all-done = bf16[2,128,1,2,128]{4,0,3,2,1:T(2,128)(2,1)S(1)} async-done(((bf16[2,128,1,2,128]{4,0,3,2,1:T(2,128)(2,1)}), bf16[2,128,1,2,128]{4,0,3,2,1:T(2,128)(2,1)S(1)}, u32[]{:S(2)}, u32[]{:S(2)}) %all-to-all-start) | async-done | bytes 131104 | tf_op jit(solution)/shard_map/all_to_all | solution.py:57
  21.6 5.5 %all-to-all-start.1 = ((bf16[8,32,1,2,128]{4,1,3,2,0:T(8,128)(2,1)}), bf16[8,32,1,2,128]{4,1,3,2,0:T(8,128)(2,1)S(1)}, u32[]{:S(2)}, u32[]{:S(2)}) async-start(bf16[8,32,1,2,128]{4,1,3,2,0:T(8,128)(2,1)} %bitcast.15), calls=%async_computation.1 | async-start | bytes 262144 | tf_op jit(solution)/shard_map/all_to_all | solution.py:56
  29.0 1.6 all-to-all-done.1
  30.7 4.9 %conditional.2 = (bf16[32,8,2,128]{3,2,1,0:T(2,128)(2,1)}) conditional(s32[]{:T(128)} %bitcast.19, bf16[32,8,2,128]{3,2,1,0:T(2,128)(2,1)S(1)} %copy.69, bf16[32,8,2,128]{3,2,1,0:T(2,128)(2,1)S(1)} %copy.69, bf16[32,8,2,128]{3,2,1,0:T(2,128)(2,1)S(1)} %copy.69, bf16[32,8,2,128]{3,2,1,0:T(2,128)(2,1)S(1)} %copy.69, ...), branch_computations={%region_1.2_spmd, %region_2.3_spmd, %region_3.4_spmd, %region_4.5_... | conditional | bytes 524336 | solution.py:72
  30.7 3.6 %collective-permute-start.1 = (bf16[32,8,2,128]{3,2,1,0:T(2,128)(2,1)S(1)}, bf16[32,8,2,128]{3,2,1,0:T(2,128)(2,1)}, u32[]{:S(2)}, u32[]{:S(2)}) collective-permute-start(bf16[32,8,2,128]{3,2,1,0:T(2,128)(2,1)S(1)} %param.1), channel_id=1, source_target_pairs={{8,0},{12,4},{16,8},{20,12},{24,16},{28,20},{9,1},{13,5},{17,9},{2... | collective-permute-start | bytes 393224 | tf_op jit(solution)/shard_map/cond/branch_1_fun/ppermute | solution.py:21
  34.3 1.3 collective-permute-done.1
  35.6 1.3 conditional.3
  35.6 1.3 collective-permute-start.13
  37.0 1.4 broadcast_select_fusion
  40.6 5.5 %convolution_bitcast_fusion = f32[2,32,2,128,128]{3,4,2,1,0:T(8,128)} fusion(bf16[2,32,16,1,128]{4,2,3,1,0:T(8,128)(2,1)S(1)} %bitcast.79, bf16[2,32,16,1,128]{4,2,3,1,0:T(8,128)(2,1)S(1)} %maximum_select_fusion, bf16[1,32,16,128]{3,2,1,0:T(8,128)(2,1)} %bitcast.30, bf16[1,32,16,128]{3,2,1,0:T(8,128)(2,1)} %bitcast.29, ...), kind=kOutput, calls=%fused_computation.2 | convolution fusion | flops 67633152 | bytes 9306114 | tf_op jit(solution)/shard_map/kfsc,kfsrd->kfrcd/dot_general | solution.py:83
  46.1 8.9 %copy.85 = f32[2,32,2,128,128]{4,3,2,1,0:T(8,128)} copy(f32[2,32,2,128,128]{3,4,2,1,0:T(8,128)} %convolution_bitcast_fusion) | data formatting | bytes 16777216 | tf_op jit(solution)/shard_map/kfsc,kfsrd->kfrcd/transpose | solution.py:83
  55.0 9.4 %reshape.414 = f32[2,64,16384]{2,1,0:T(8,128)} reshape(f32[2,32,2,128,128]{4,3,2,1,0:T(8,128)} %copy.85) | data formatting | bytes 16777216 | tf_op jit(solution)/shard_map/reshape | solution.py:86
  64.4 6.4 %fusion = bf16[2,4,8,16384]{3,2,1,0:T(8,128)(2,1)S(1)} fusion(f32[32,64,1]{0,1,2:T(8,128)S(1)} %bitcast.81, f32[2,64,16384]{2,1,0:T(8,128)} %reshape.414), kind=kOutput, calls=%fused_computation.1 | convolution fusion | flops 806354944 | bytes 10493952 | tf_op jit(solution)/shard_map/lq,kqx->lkx/dot_general | solution.py:97
  70.9 1.5 copy.97
  72.4 42.0 %reduce-scatter.4.cloned.1.call-done = bf16[8,32768]{1,0:T(8,128)(2,1)} async-done(((bf16[32,32768]{1,0:T(8,128)(2,1)}), bf16[8,32768]{1,0:T(8,128)(2,1)}) %reduce-scatter.4.cloned.1.call-update) | async-done | bytes 524304
  114.4 1.2 copy.87
  115.6 3.1 %collective-permute-start.14 = (bf16[2,8,128,128]{3,2,1,0:T(8,128)(2,1)S(1)}, bf16[2,8,128,128]{3,2,1,0:T(8,128)(2,1)S(1)}, u32[]{:S(2)}, u32[]{:S(2)}) collective-permute-start(bf16[2,8,128,128]{3,2,1,0:T(8,128)(2,1)S(1)} %copy.87), channel_id=1, source_target_pairs={{0,4},{4,8},{8,12},{12,16},{16,20},{20,24},{24,28},{1,5},{5,9},{9,... | collective-permute-start | bytes 1572872 | tf_op jit(solution)/shard_map/ppermute | solution.py:21
  118.8 12.3 %collective-permute-done.14 = bf16[2,8,128,128]{3,2,1,0:T(8,128)(2,1)S(1)} collective-permute-done((bf16[2,8,128,128]{3,2,1,0:T(8,128)(2,1)S(1)}, bf16[2,8,128,128]{3,2,1,0:T(8,128)(2,1)S(1)}, u32[]{:S(2)}, u32[]{:S(2)}) %collective-permute-start.14) | collective-permute-done | bytes 524320 | tf_op jit(solution)/shard_map/ppermute | solution.py:21
  132.2 1.3 collective-permute-start.15
  133.5 12.4 %collective-permute-done.15 = bf16[2,8,128,128]{3,2,1,0:T(8,128)(2,1)S(1)} collective-permute-done((bf16[2,8,128,128]{3,2,1,0:T(8,128)(2,1)S(1)}, bf16[2,8,128,128]{3,2,1,0:T(8,128)(2,1)S(1)}, u32[]{:S(2)}, u32[]{:S(2)}) %collective-permute-start.15) | collective-permute-done | bytes 524320 | tf_op jit(solution)/shard_map/ppermute | solution.py:21
  146.0 1.3 collective-permute-start.16
  148.2 25.7 %collective-permute-done.16 = bf16[2,8,128,128]{3,2,1,0:T(8,128)(2,1)S(1)} collective-permute-done((bf16[2,8,128,128]{3,2,1,0:T(8,128)(2,1)S(1)}, bf16[2,8,128,128]{3,2,1,0:T(8,128)(2,1)S(1)}, u32[]{:S(2)}, u32[]{:S(2)}) %collective-permute-start.16) | collective-permute-done | bytes 524320 | tf_op jit(solution)/shard_map/ppermute | solution.py:21
  (37 shorter events, 8.9 us)
Async XLA Ops:
  7.2 4.4 %copy-start = (bf16[1,256,2048]{2,1,0:T(8,128)(2,1)S(1)}, bf16[1,256,2048]{2,1,0:T(8,128)(2,1)}, u32[]{:S(2)}) copy-start(bf16[1,256,2048]{2,1,0:T(8,128)(2,1)} %param.17) | copy-start | bytes 3145732
  11.6 15.5 %copy-start.2 = (s32[2]{0:T(128)S(1)}, s32[2]{0:T(128)}, u32[]{:S(2)}) copy-start(s32[2]{0:T(128)} %param.18) | copy-start | bytes 28
  11.6 17.4 %copy-start.3 = (s32[1,2]{1,0:T(1,128)S(1)}, s32[1,2]{1,0:T(1,128)}, u32[]{:S(2)}) copy-start(s32[1,2]{1,0:T(1,128)} %param.19) | copy-start | bytes 28
  13.4 7.5 %all-to-all-start = ((bf16[2,128,1,2,128]{4,0,3,2,1:T(2,128)(2,1)}), bf16[2,128,1,2,128]{4,0,3,2,1:T(2,128)(2,1)S(1)}, u32[]{:S(2)}, u32[]{:S(2)}) async-start(bf16[2,128,1,2,128]{4,0,3,2,1:T(2,128)(2,1)} %copy.65), calls=%async_computation | async-start | bytes 262144 | tf_op jit(solution)/shard_map/all_to_all | solution.py:57
  21.6 8.9 %all-to-all-start.1 = ((bf16[8,32,1,2,128]{4,1,3,2,0:T(8,128)(2,1)}), bf16[8,32,1,2,128]{4,1,3,2,0:T(8,128)(2,1)S(1)}, u32[]{:S(2)}, u32[]{:S(2)}) async-start(bf16[8,32,1,2,128]{4,1,3,2,0:T(8,128)(2,1)} %bitcast.15), calls=%async_computation.1 | async-start | bytes 262144 | tf_op jit(solution)/shard_map/all_to_all | solution.py:56
  27.1 87.3 %reduce-scatter.4.cloned.1.call-start = ((), (), s32[]{:S(2)}) async-start(), calls=%async_computation.3 | async-start | bytes 2621440
  30.7 4.9 %collective-permute-start.1 = (bf16[32,8,2,128]{3,2,1,0:T(2,128)(2,1)S(1)}, bf16[32,8,2,128]{3,2,1,0:T(2,128)(2,1)}, u32[]{:S(2)}, u32[]{:S(2)}) collective-permute-start(bf16[32,8,2,128]{3,2,1,0:T(2,128)(2,1)S(1)} %param.1), channel_id=1, source_target_pairs={{8,0},{12,4},{16,8},{20,12},{24,16},{28,20},{9,1},{13,5},{17,9},{2... | collective-permute-start | bytes 393224 | tf_op jit(solution)/shard_map/cond/branch_1_fun/ppermute | solution.py:21
  35.6 1.3 collective-permute-start.13
  114.4 32.9 %copy-start.1 = (bf16[8,32768]{1,0:T(8,128)(2,1)S(1)}, bf16[8,32768]{1,0:T(8,128)(2,1)}, u32[]{:S(2)}) copy-start(bf16[8,32768]{1,0:T(8,128)(2,1)} %reduce-scatter.4.cloned.1.call-done) | copy-start | bytes 1572868
  115.6 15.4 %collective-permute-start.14 = (bf16[2,8,128,128]{3,2,1,0:T(8,128)(2,1)S(1)}, bf16[2,8,128,128]{3,2,1,0:T(8,128)(2,1)S(1)}, u32[]{:S(2)}, u32[]{:S(2)}) collective-permute-start(bf16[2,8,128,128]{3,2,1,0:T(8,128)(2,1)S(1)} %copy.87), channel_id=1, source_target_pairs={{0,4},{4,8},{8,12},{12,16},{16,20},{20,24},{24,28},{1,5},{5,9},{9,... | collective-permute-start | bytes 1572872 | tf_op jit(solution)/shard_map/ppermute | solution.py:21
  132.2 13.7 %collective-permute-start.15 = (bf16[2,8,128,128]{3,2,1,0:T(8,128)(2,1)S(1)}, bf16[2,8,128,128]{3,2,1,0:T(8,128)(2,1)S(1)}, u32[]{:S(2)}, u32[]{:S(2)}) collective-permute-start(bf16[2,8,128,128]{3,2,1,0:T(8,128)(2,1)S(1)} %broadcast_select_fusion.1), channel_id=1, source_target_pairs={{0,8},{4,12},{8,16},{12,20},{16,24},{20,28},{1,9},{5,13},{9,17},{1... | collective-permute-start | bytes 1572872 | tf_op jit(solution)/shard_map/ppermute | solution.py:21
  146.0 27.9 %collective-permute-start.16 = (bf16[2,8,128,128]{3,2,1,0:T(8,128)(2,1)S(1)}, bf16[2,8,128,128]{3,2,1,0:T(8,128)(2,1)S(1)}, u32[]{:S(2)}, u32[]{:S(2)}) collective-permute-start(bf16[2,8,128,128]{3,2,1,0:T(8,128)(2,1)S(1)} %broadcast_select_fusion.2), channel_id=1, source_target_pairs={{0,16},{4,20},{8,24},{12,28},{1,17},{5,21},{9,25},{13,29},{2,18},{... | collective-permute-start | bytes 1572872 | tf_op jit(solution)/shard_map/ppermute | solution.py:21
Sparse Core Ops, SparseCore 0:
  72.5 41.8 reduce-scatter.3
where the time goes:
time: 183 us; the launch traced here: 182 us
  waiting for transfers between devices  98.6 us (54%)
  local copies, waits for them, and re-layouts  24.2 us (13%)
  starting transfers between devices  20 us (11%)
  between operations  15.4 us (8%)
  matrix products  12.9 us (7%)
  other arithmetic  10.4 us (6%)
    ppermute x5, waiting for transfers between devices, shifted_2(): lax.ppermute(value, axis, [(source, source + steps) for source in range(l...  51.6 us
    unnamed x2, waiting for transfers between devices  42 us
    ppermute x5, starting transfers between devices, shifted_2(): lax.ppermute(value, axis, [(source, source + steps) for source in range(l...  10.6 us
    reshape x1, local copies, waits for them, and re-layouts, local(): cross_rows = cross.reshape(offset_total, 2 * bin_local, BLOCK_CH * BLOCK_CH)  9.44 us
    transpose x1, local copies, waits for them, and re-layouts, local(): jnp.einsum('kfsc,kfsrd->kfrcd', left_side, right_side, preferred_element_...  8.89 us
    dot_general x1, matrix products, local(): jnp.einsum('lq,kqx->lkx', lag_table, cross_rows, precision=lax.Precision....  6.43 us
    dot_general x1, matrix products, local(): jnp.einsum('kfsc,kfsrd->kfrcd', left_side, right_side, preferred_element_...  5.54 us
    all_to_all x1, starting transfers between devices, local(): lax.all_to_all(lax.all_to_all(whitened, 'pair', split_axis=1, concat_axis...  5.46 us
  transfers between devices with their start and end apart: 8, of which 7 were waited for; matrix products, arithmetic and copies ran while one was open for 1% of the time, Pallas kernels for 0%

commit v1 on v0

--- a/solution.py
+++ b/solution.py
@@ -9,6 +9,15 @@
 SAMPLES = 2048
 FIRST_BIN = 4
 LAGS = 32
+divide_the_tails = lambda vector: jnp.concatenate(
+    lax.all_to_all(
+        jnp.stack(jnp.split(vector, lax.axis_size("blk"), axis=0)),
+        axis_name="blk",
+        split_axis=0,
+        concat_axis=0,
+    ),
+    axis=2,
+)
 
 
 def as_sent(value):
@@ -53,12 +62,8 @@
     band_level = jnp.mean(band_power, axis=-1)
     whiten_scale = 1.0 / jnp.sqrt(band_level + 1e-05)
     whitened = (spectrum * whiten_scale[:, :, :, None, None]).astype(jnp.bfloat16)
-    regrouped = lax.all_to_all(
-        lax.all_to_all(whitened, "pair", split_axis=1, concat_axis=0, tiled=True),
-        "blk",
-        split_axis=0,
-        concat_axis=2,
-        tiled=True,
+    regrouped = divide_the_tails(
+        lax.all_to_all(whitened, "pair", split_axis=1, concat_axis=0, tiled=True)
     )
     own_block = regrouped[0]
     bin_local = own_block.shape[0]

time: 183 us -> 187 us (1.022)
  local copies, waits for them, and re-layouts: 24.2 us -> 28.4 us
    unnamed x10 -> x17, local copies, waits for them, and re-layouts: 2.42 us -> 6.67 us
where the time goes in v1:
time: 187 us; the launch traced here: 186 us
  waiting for transfers between devices  98.6 us (53%)
  local copies, waits for them, and re-layouts  28.4 us (15%)
  starting transfers between devices  20 us (11%)
  between operations  15.4 us (8%)
  matrix products  12.9 us (7%)
  other arithmetic  10.4 us (6%)
    ppermute x5, waiting for transfers between devices, shifted_2(): lax.ppermute(value, axis, [(source, source + steps) for source in range(l...  51.6 us
    unnamed x2, waiting for transfers between devices  42 us
    ppermute x5, starting transfers between devices, shifted_2(): lax.ppermute(value, axis, [(source, source + steps) for source in range(l...  10.6 us
    reshape x1, local copies, waits for them, and re-layouts, local(): cross_rows = cross.reshape(offset_total, 2 * bin_local, BLOCK_CH * BLOCK_CH)  9.44 us
    transpose x1, local copies, waits for them, and re-layouts, local(): jnp.einsum('kfsc,kfsrd->kfrcd', left_side, right_side, preferred_element_...  8.89 us
    unnamed x17, local copies, waits for them, and re-layouts  6.67 us
    dot_general x1, matrix products, local(): jnp.einsum('lq,kqx->lkx', lag_table, cross_rows, precision=lax.Precision....  6.43 us
    dot_general x1, matrix products, local(): jnp.einsum('kfsc,kfsrd->kfrcd', left_side, right_side, preferred_element_...  5.54 us
  transfers between devices with their start and end apart: 8, of which 7 were waited for; matrix products, arithmetic and copies ran while one was open for 1% of the time, Pallas kernels for 0%

profile of v1, /device:TPU:25, one launch (start us, length us, event | category | flops | bytes accessed | tf_op | source)
XLA Modules:
  0.0 185.8 jit_solution(17263714962167585406)
XLA Ops:
  7.2 4.2 %cosine_multiply_fusion = (f32[2048,128,1]{1,0,2:T(8,128)S(1)}, f32[2048,128,1]{1,0,2:T(8,128)S(1)}) fusion(s32[128]{0:T(128)S(1)} %iota_add_fusion, f32[2048]{0:T(1024)S(1)} %get-tuple-element.57, f32[2048]{0:T(1024)S(1)} %get-tuple-element.58), kind=kLoop, calls=%fused_computation.18 | loop fusion | flops 4194304 | bytes 2114048 | tf_op jit(solution)/shard_map/mul | solution.py:40
  13.4 4.0 %all-to-all-start = ((bf16[2,128,1,2,128]{4,0,3,2,1:T(2,128)(2,1)}), bf16[2,128,1,2,128]{4,0,3,2,1:T(2,128)(2,1)S(1)}, u32[]{:S(2)}, u32[]{:S(2)}) async-start(bf16[2,128,1,2,128]{4,0,3,2,1:T(2,128)(2,1)} %copy.79), calls=%async_computation | async-start | bytes 262144 | tf_op jit(solution)/shard_map/all_to_all | solution.py:66
  17.6 3.4 %all-to-all-done = bf16[2,128,1,2,128]{4,0,3,2,1:T(2,128)(2,1)S(1)} async-done(((bf16[2,128,1,2,128]{4,0,3,2,1:T(2,128)(2,1)}), bf16[2,128,1,2,128]{4,0,3,2,1:T(2,128)(2,1)S(1)}, u32[]{:S(2)}, u32[]{:S(2)}) %all-to-all-start) | async-done | bytes 131104 | tf_op jit(solution)/shard_map/all_to_all | solution.py:66
  25.8 5.5 %all-to-all-start.1 = ((bf16[8,1,32,1,2,128]{5,2,4,3,1,0:T(8,128)(2,1)}), bf16[8,1,32,1,2,128]{5,2,4,3,1,0:T(8,128)(2,1)S(1)}, u32[]{:S(2)}, u32[]{:S(2)}) async-start(bf16[8,1,32,1,2,128]{5,2,4,3,1,0:T(8,128)(2,1)} %constant_dynamic-update-slice_fusion), calls=%async_computation.1 | async-start | bytes 262144 | tf_op jit(solution)/shard_map/all_to_all | solution.py:13
  33.2 1.6 all-to-all-done.1
  34.9 4.9 %conditional.2 = (bf16[32,8,2,128]{3,2,1,0:T(2,128)(2,1)}) conditional(s32[]{:T(128)} %bitcast.26, bf16[32,8,2,128]{3,2,1,0:T(2,128)(2,1)S(1)} %copy.83, bf16[32,8,2,128]{3,2,1,0:T(2,128)(2,1)S(1)} %copy.83, bf16[32,8,2,128]{3,2,1,0:T(2,128)(2,1)S(1)} %copy.83, bf16[32,8,2,128]{3,2,1,0:T(2,128)(2,1)S(1)} %copy.83, ...), branch_computations={%region_1.2_spmd, %region_2.3_spmd, %region_3.4_spmd, %region_4.5_... | conditional | bytes 524336 | solution.py:77
  34.9 3.6 %collective-permute-start.1 = (bf16[32,8,2,128]{3,2,1,0:T(2,128)(2,1)S(1)}, bf16[32,8,2,128]{3,2,1,0:T(2,128)(2,1)}, u32[]{:S(2)}, u32[]{:S(2)}) collective-permute-start(bf16[32,8,2,128]{3,2,1,0:T(2,128)(2,1)S(1)} %param.1), channel_id=1, source_target_pairs={{8,0},{12,4},{16,8},{20,12},{24,16},{28,20},{9,1},{13,5},{17,9},{2... | collective-permute-start | bytes 393224 | tf_op jit(solution)/shard_map/cond/branch_1_fun/ppermute | solution.py:30
  38.5 1.3 collective-permute-done.1
  39.8 1.3 conditional.3
  39.8 1.3 collective-permute-start.13
  41.2 1.4 broadcast_select_fusion
  44.8 5.5 %convolution_bitcast_fusion = f32[2,32,2,128,128]{3,4,2,1,0:T(8,128)} fusion(bf16[2,32,16,1,128]{4,2,3,1,0:T(8,128)(2,1)S(1)} %bitcast.109, bf16[2,32,16,1,128]{4,2,3,1,0:T(8,128)(2,1)S(1)} %maximum_select_fusion, bf16[1,32,16,128]{3,2,1,0:T(8,128)(2,1)} %bitcast.36, bf16[1,32,16,128]{3,2,1,0:T(8,128)(2,1)} %bitcast.35, ...), kind=kOutput, calls=%fused_computation.2 | convolution fusion | flops 67633152 | bytes 9306114 | tf_op jit(solution)/shard_map/kfsc,kfsrd->kfrcd/dot_general | solution.py:88
  50.3 8.9 %copy.99 = f32[2,32,2,128,128]{4,3,2,1,0:T(8,128)} copy(f32[2,32,2,128,128]{3,4,2,1,0:T(8,128)} %convolution_bitcast_fusion) | data formatting | bytes 16777216 | tf_op jit(solution)/shard_map/kfsc,kfsrd->kfrcd/transpose | solution.py:88
  59.2 9.4 %reshape.417 = f32[2,64,16384]{2,1,0:T(8,128)} reshape(f32[2,32,2,128,128]{4,3,2,1,0:T(8,128)} %copy.99) | data formatting | bytes 16777216 | tf_op jit(solution)/shard_map/reshape | solution.py:91
  68.6 6.4 %fusion = bf16[2,4,8,16384]{3,2,1,0:T(8,128)(2,1)S(1)} fusion(f32[32,64,1]{0,1,2:T(8,128)S(1)} %bitcast.119, f32[2,64,16384]{2,1,0:T(8,128)} %reshape.417), kind=kOutput, calls=%fused_computation.1 | convolution fusion | flops 806354944 | bytes 10493952 | tf_op jit(solution)/shard_map/lq,kqx->lkx/dot_general | solution.py:102
  75.1 1.5 copy.111
  76.6 42.0 %reduce-scatter.4.cloned.1.call-done = bf16[8,32768]{1,0:T(8,128)(2,1)} async-done(((bf16[32,32768]{1,0:T(8,128)(2,1)}), bf16[8,32768]{1,0:T(8,128)(2,1)}) %reduce-scatter.4.cloned.1.call-update) | async-done | bytes 524304
  118.6 1.2 copy.101
  119.8 3.1 %collective-permute-start.14 = (bf16[2,8,128,128]{3,2,1,0:T(8,128)(2,1)S(1)}, bf16[2,8,128,128]{3,2,1,0:T(8,128)(2,1)S(1)}, u32[]{:S(2)}, u32[]{:S(2)}) collective-permute-start(bf16[2,8,128,128]{3,2,1,0:T(8,128)(2,1)S(1)} %copy.101), channel_id=1, source_target_pairs={{0,4},{4,8},{8,12},{12,16},{16,20},{20,24},{24,28},{1,5},{5,9},{9,... | collective-permute-start | bytes 1572872 | tf_op jit(solution)/shard_map/ppermute | solution.py:30
  123.0 12.3 %collective-permute-done.14 = bf16[2,8,128,128]{3,2,1,0:T(8,128)(2,1)S(1)} collective-permute-done((bf16[2,8,128,128]{3,2,1,0:T(8,128)(2,1)S(1)}, bf16[2,8,128,128]{3,2,1,0:T(8,128)(2,1)S(1)}, u32[]{:S(2)}, u32[]{:S(2)}) %collective-permute-start.14) | collective-permute-done | bytes 524320 | tf_op jit(solution)/shard_map/ppermute | solution.py:30
  136.4 1.3 collective-permute-start.15
  137.7 12.4 %collective-permute-done.15 = bf16[2,8,128,128]{3,2,1,0:T(8,128)(2,1)S(1)} collective-permute-done((bf16[2,8,128,128]{3,2,1,0:T(8,128)(2,1)S(1)}, bf16[2,8,128,128]{3,2,1,0:T(8,128)(2,1)S(1)}, u32[]{:S(2)}, u32[]{:S(2)}) %collective-permute-start.15) | collective-permute-done | bytes 524320 | tf_op jit(solution)/shard_map/ppermute | solution.py:30
  150.2 1.3 collective-permute-start.16
  152.4 25.6 %collective-permute-done.16 = bf16[2,8,128,128]{3,2,1,0:T(8,128)(2,1)S(1)} collective-permute-done((bf16[2,8,128,128]{3,2,1,0:T(8,128)(2,1)S(1)}, bf16[2,8,128,128]{3,2,1,0:T(8,128)(2,1)S(1)}, u32[]{:S(2)}, u32[]{:S(2)}) %collective-permute-start.16) | collective-permute-done | bytes 524320 | tf_op jit(solution)/shard_map/ppermute | solution.py:30
  (45 shorter events, 13.1 us)
Async XLA Ops:
  7.2 4.4 %copy-start = (bf16[1,256,2048]{2,1,0:T(8,128)(2,1)S(1)}, bf16[1,256,2048]{2,1,0:T(8,128)(2,1)}, u32[]{:S(2)}) copy-start(bf16[1,256,2048]{2,1,0:T(8,128)(2,1)} %param.17) | copy-start | bytes 3145732
  11.6 19.7 %copy-start.2 = (s32[2]{0:T(128)S(1)}, s32[2]{0:T(128)}, u32[]{:S(2)}) copy-start(s32[2]{0:T(128)} %param.18) | copy-start | bytes 28
  11.6 21.6 %copy-start.3 = (s32[1,2]{1,0:T(1,128)S(1)}, s32[1,2]{1,0:T(1,128)}, u32[]{:S(2)}) copy-start(s32[1,2]{1,0:T(1,128)} %param.19) | copy-start | bytes 28
  13.4 7.5 %all-to-all-start = ((bf16[2,128,1,2,128]{4,0,3,2,1:T(2,128)(2,1)}), bf16[2,128,1,2,128]{4,0,3,2,1:T(2,128)(2,1)S(1)}, u32[]{:S(2)}, u32[]{:S(2)}) async-start(bf16[2,128,1,2,128]{4,0,3,2,1:T(2,128)(2,1)} %copy.79), calls=%async_computation | async-start | bytes 262144 | tf_op jit(solution)/shard_map/all_to_all | solution.py:66
  25.8 8.9 %all-to-all-start.1 = ((bf16[8,1,32,1,2,128]{5,2,4,3,1,0:T(8,128)(2,1)}), bf16[8,1,32,1,2,128]{5,2,4,3,1,0:T(8,128)(2,1)S(1)}, u32[]{:S(2)}, u32[]{:S(2)}) async-start(bf16[8,1,32,1,2,128]{5,2,4,3,1,0:T(8,128)(2,1)} %constant_dynamic-update-slice_fusion), calls=%async_computation.1 | async-start | bytes 262144 | tf_op jit(solution)/shard_map/all_to_all | solution.py:13
  31.3 87.3 %reduce-scatter.4.cloned.1.call-start = ((), (), s32[]{:S(2)}) async-start(), calls=%async_computation.3 | async-start | bytes 2621440
  34.9 4.9 %collective-permute-start.1 = (bf16[32,8,2,128]{3,2,1,0:T(2,128)(2,1)S(1)}, bf16[32,8,2,128]{3,2,1,0:T(2,128)(2,1)}, u32[]{:S(2)}, u32[]{:S(2)}) collective-permute-start(bf16[32,8,2,128]{3,2,1,0:T(2,128)(2,1)S(1)} %param.1), channel_id=1, source_target_pairs={{8,0},{12,4},{16,8},{20,12},{24,16},{28,20},{9,1},{13,5},{17,9},{2... | collective-permute-start | bytes 393224 | tf_op jit(solution)/shard_map/cond/branch_1_fun/ppermute | solution.py:30
  39.8 1.3 collective-permute-start.13
  118.6 32.9 %copy-start.1 = (bf16[8,32768]{1,0:T(8,128)(2,1)S(1)}, bf16[8,32768]{1,0:T(8,128)(2,1)}, u32[]{:S(2)}) copy-start(bf16[8,32768]{1,0:T(8,128)(2,1)} %reduce-scatter.4.cloned.1.call-done) | copy-start | bytes 1572868
  119.8 15.4 %collective-permute-start.14 = (bf16[2,8,128,128]{3,2,1,0:T(8,128)(2,1)S(1)}, bf16[2,8,128,128]{3,2,1,0:T(8,128)(2,1)S(1)}, u32[]{:S(2)}, u32[]{:S(2)}) collective-permute-start(bf16[2,8,128,128]{3,2,1,0:T(8,128)(2,1)S(1)} %copy.101), channel_id=1, source_target_pairs={{0,4},{4,8},{8,12},{12,16},{16,20},{20,24},{24,28},{1,5},{5,9},{9,... | collective-permute-start | bytes 1572872 | tf_op jit(solution)/shard_map/ppermute | solution.py:30
  136.4 13.7 %collective-permute-start.15 = (bf16[2,8,128,128]{3,2,1,0:T(8,128)(2,1)S(1)}, bf16[2,8,128,128]{3,2,1,0:T(8,128)(2,1)S(1)}, u32[]{:S(2)}, u32[]{:S(2)}) collective-permute-start(bf16[2,8,128,128]{3,2,1,0:T(8,128)(2,1)S(1)} %broadcast_select_fusion.1), channel_id=1, source_target_pairs={{0,8},{4,12},{8,16},{12,20},{16,24},{20,28},{1,9},{5,13},{9,17},{1... | collective-permute-start | bytes 1572872 | tf_op jit(solution)/shard_map/ppermute | solution.py:30
  150.2 27.8 %collective-permute-start.16 = (bf16[2,8,128,128]{3,2,1,0:T(8,128)(2,1)S(1)}, bf16[2,8,128,128]{3,2,1,0:T(8,128)(2,1)S(1)}, u32[]{:S(2)}, u32[]{:S(2)}) collective-permute-start(bf16[2,8,128,128]{3,2,1,0:T(8,128)(2,1)S(1)} %broadcast_select_fusion.2), channel_id=1, source_target_pairs={{0,16},{4,20},{8,24},{12,28},{1,17},{5,21},{9,25},{13,29},{2,18},{... | collective-permute-start | bytes 1572872 | tf_op jit(solution)/shard_map/ppermute | solution.py:30
Sparse Core Ops, SparseCore 0:
  76.7 41.8 reduce-scatter.3
